TPU v7x, 32 devices: a whole 2x2x4 slice. The times are simulated.
32 devices in a mesh: grp: 8 (over z, core), blk: 4 (over y, x).
Axes of the slice: x: 2, y: 2, z: 4, core: 2. Of those that a mesh axis runs over, the one named last changes fastest.
Arguments:
- slab: bfloat16 [2048, 32768], P(('grp', 'blk')), as said below
- pick_owner: int32 [2048, 1], P(('grp', 'blk')), may hold values from 0 to 3; in each aligned block of 64 rows (0 to 63, 64 to 127, ...) at most 32 rows name the same one
- pick_offset: int32 [2048], P(('grp', 'blk')), may hold values from 0 to 63
- wedge_id: int32 [2048], P(('grp', 'blk')), may hold values from 0 to 7
- live_count: int32 [32], P(('grp', 'blk')), may hold values from 16 to 64, as said below
- references: bfloat16 [192, 32768], P('blk')
- wedge: float32 [8, 32768], replicated, may hold values from 0.05 to 1
Outputs:
- new_refs: float32 [192, 32768], P('blk', 'grp')
Inputs may be any that keep to these rules, and one draw needn't show every extreme that they name: `pick_owner`: on one device at most 32 slots name the same owner. `live_count`: live slots are the first ones of a device; some device has all 64 live. `slab`: coefficients of the tomogram blocks.
All inputs are finite; a program needn't handle non-finite values.
Results may differ from a plain program's by a relative error of at most 0.0036.
Values may be sent and summed in bfloat16 or wider, within the bound.
No kernel may reach another device: no remote copies, remote signals or barrier semaphores. Data moves between devices by JAX's collectives and lax.ppermute only.
A program may use at most 128 MiB of HBM per device.

v0:
```python
import math
import jax
import jax.numpy as jnp
from jax import lax
from jax.sharding import PartitionSpec as P


def per_device(slab, pick_owner, pick_offset, wedge_id, live_count, references, wedge):
    highest = lax.Precision.HIGHEST
    slot_count, voxels = slab.shape
    group_count = lax.axis_size("grp")
    cycle_size = lax.axis_size("blk")
    capacity = 2 * slot_count // cycle_size
    owners = pick_owner[:, 0]
    owner_hot = (owners[:, None] == jnp.arange(cycle_size, dtype=jnp.int32)[None, :]).astype(
        jnp.int32
    )
    slot_rank = jnp.sum((jnp.cumsum(owner_hot, axis=0) - 1) * owner_hot, axis=1)
    requests = jnp.zeros((cycle_size, capacity), jnp.int32).at[owners, slot_rank].set(pick_offset)
    wanted = lax.all_to_all(requests, "blk", split_axis=0, concat_axis=0, tiled=True)
    amount = wanted.shape[1]
    blocks_out = jnp.take(slab, wanted.reshape(-1), axis=0).reshape(cycle_size, amount, voxels)
    fetched = lax.all_to_all(blocks_out, "blk", split_axis=0, concat_axis=0, tiled=True)
    blocks = fetched[owners, slot_rank]
    masks_hot = (wedge_id[:, None] == jnp.arange(wedge.shape[0], dtype=jnp.int32)[None, :]).astype(
        jnp.float32
    )
    weights = jnp.dot(masks_hot, wedge, precision=highest)
    scaled = (weights * blocks.astype(jnp.float32)).astype(jnp.bfloat16)
    per_ref = references.shape[0]
    inv_noise = 1.0 / (32.0 * math.sqrt(voxels))
    ref_piece = lax.all_gather(references, "blk", axis=0, tiled=True)
    correl = jnp.dot(scaled, ref_piece.T, preferred_element_type=jnp.float32)
    piece_float = ref_piece.astype(jnp.float32)
    piece_norms = jnp.dot(wedge, (piece_float * piece_float).T, precision=highest)
    chosen_norms = jnp.dot(masks_hot, piece_norms, precision=highest)
    folded = correl - 0.5 * chosen_norms
    posterior = jax.nn.softmax(folded * inv_noise, axis=1)
    live_mask = (jnp.arange(slot_count, dtype=jnp.int32) < live_count[0]).astype(jnp.float32)
    weighted = posterior * live_mask[:, None]
    weighted_b = weighted.astype(jnp.bfloat16)
    totals = lax.psum(jnp.dot(weighted.T, masks_hot, precision=highest), ("grp", "blk"))
    per_vox = voxels // group_count
    contract = (((0,), (0,)), ((), ()))
    columns = lax.all_to_all(scaled, "grp", split_axis=1, concat_axis=0, tiled=True)
    all_weights = lax.all_gather(weighted_b, "grp", axis=0, tiled=True)
    summed = lax.psum_scatter(
        lax.dot_general(all_weights, columns, contract, preferred_element_type=jnp.float32),
        "blk",
        scatter_dimension=0,
        tiled=True,
    )
    row_first = lax.axis_index("blk") * per_ref
    vox_first = lax.axis_index("grp") * per_vox
    own_totals = lax.dynamic_slice_in_dim(totals, row_first, per_ref, 0)
    wedge_cols = lax.dynamic_slice_in_dim(wedge, vox_first, per_vox, 1)
    weight_sum = jnp.dot(own_totals, wedge_cols, precision=highest)
    return summed / (weight_sum + 1.0)


def solution(mesh):
    placed = (
        P(("grp", "blk"), None),
        P(("grp", "blk"), None),
        P(("grp", "blk")),
        P(("grp", "blk")),
        P(("grp", "blk")),
        P("blk", None),
        P(),
    )
    return jax.shard_map(
        per_device, mesh=mesh, in_specs=placed, out_specs=P("blk", "grp"), check_vma=False
    )
```

profile of v0, /device:TPU:0, one launch (start us, length us, event | category | flops | bytes accessed | tf_op | source)
XLA Modules:
  0.0 415.6 jit_solution(10837172099122750557)
XLA Ops:
  6.5 0.0 copy-start
  6.5 0.8 fusion.9
  7.4 0.1 reduce_window_sum.11
  7.4 0.8 select_reduce_fusion
  8.3 0.7 fusion.18
  9.0 0.6 broadcast_in_dim.12
  9.5 10.1 %scatter_fusion = s32[4,32]{1,0:T(4,128)} fusion(s32[4,32]{1,0:T(4,128)} %broadcast_in_dim.12, s32[64]{0:T(128)S(1)} %get-tuple-element.7, s32[64]{0:T(128)} %param.9), kind=kCustom, calls=%fused_computation.2 | custom fusion | bytes 1280 | tf_op jit(solution)/shard_map/scatter | solution.py:19
  19.7 5.2 %all-to-all-start = ((s32[4,1,32]{2,1,0:T(1,128)}), s32[4,1,32]{2,1,0:T(1,128)S(1)}, u32[]{:S(2)}, u32[]{:S(2)}) async-start(s32[4,1,32]{2,1,0:T(1,128)} %bitcast.4), calls=%async_computation | async-start | bytes 4096 | tf_op jit(solution)/shard_map/all_to_all | solution.py:20
  24.9 0.0 all-gather.2.cloned.1.call-start
  24.9 0.7 all-gather.2.cloned.1.call-update
  25.6 3.9 all-to-all-done
  29.5 0.5 broadcast.140
  30.0 0.7 reduce.3
  30.6 0.1 reshape.75
  30.7 19.2 %gather_fusion = bf16[128,32768]{1,0:T(8,128)(2,1)} fusion(bf16[64,32768]{1,0:T(8,128)(2,1)} %param.7, s32[1024]{0:T(1024)S(1)} %pad_clamp_fusion), kind=kCustom, calls=%fused_computation | custom fusion | bytes 16777728 | tf_op jit(solution)/shard_map/jit(_take)/gather | solution.py:22
  49.9 7.4 %broadcast_select_fusion = bf16[4,32,32768]{2,1,0:T(8,128)(2,1)} fusion(bf16[4,32,32768]{2,1,0:T(8,128)(2,1)} %bitcast.36, pred[4,32]{1,0:T(4,128)(4,1)S(1)} %compare_and_fusion), kind=kLoop, calls=%fused_computation.8 | loop fusion | flops 4194304 | bytes 16777344 | tf_op jit(solution)/shard_map/jit(_take)/select_n | solution.py:22
  57.4 171.9 %all_to_all.33 = bf16[4,32,32768]{2,1,0:T(8,128)(2,1)} all-to-all(bf16[4,32,32768]{2,1,0:T(8,128)(2,1)} %broadcast_select_fusion), channel_id=1, replica_groups=mesh['grp'=8,'blk'=4] {'blk'}, dimensions={0} | all-to-all | bytes 16777216 | tf_op jit(solution)/shard_map/all_to_all | solution.py:23
  229.3 0.0 copy-start.3
  229.3 12.2 %gather_fusion.1 = bf16[64,32768]{1,0:T(8,128)(2,1)} fusion(bf16[4,32,32768]{2,1,0:T(8,128)(2,1)} %all_to_all.33, s32[64]{0:T(128)S(1)} %bitcast.38), kind=kCustom, calls=%fused_computation.1 | custom fusion | bytes 8389120 | tf_op jit(solution)/shard_map/gather | solution.py:24
  241.5 0.0 copy-done
  241.5 0.0 copy-done.3
  241.5 5.5 %fusion = bf16[64,32768]{1,0:T(8,128)(2,1)S(1)} fusion(f32[8,32768]{1,0:T(8,128)S(1)} %copy-done, bf16[64,32768]{1,0:T(8,128)(2,1)} %gather_fusion.1, s32[64]{0:T(128)S(1)} %copy-done.3), kind=kOutput, calls=%fused_computation.4 | convolution fusion | flops 207618560 | bytes 9437440 | tf_op jit(solution)/shard_map/dot_general | solution.py:28
  247.0 0.0 copy-start.1
  247.0 2.0 copy-done.1
  249.0 2.2 copy.13
  251.2 4.6 %all-to-all-start.2 = ((bf16[64,8,4096]{2,0,1:T(8,128)(2,1)}), bf16[64,8,4096]{2,0,1:T(8,128)(2,1)}, u32[]{:S(2)}, u32[]{:S(2)}) async-start(bf16[64,8,4096]{2,0,1:T(8,128)(2,1)} %bitcast.37), calls=%async_computation.2 | async-start | bytes 8388608 | tf_op jit(solution)/shard_map/all_to_all | solution.py:45
  255.8 0.3 reduce-scatter.2.cloned.1.call-start
  256.7 0.0 all-gather.2.cloned.1.call-done
  256.7 0.0 copy-start.2
  256.7 22.6 %fusion.1 = f32[192,8]{0,1:T(8,128)S(1)} fusion(f32[8,32768]{1,0:T(8,128)S(1)} %copy-done, bf16[192,32768]{1,0:T(8,128)(2,1)} %all-gather.2.cloned.1.call-done), kind=kOutput, calls=%fused_computation.5 | convolution fusion | flops 616562688 | bytes 13637632 | tf_op jit(solution)/shard_map/dot_general | solution.py:35
  279.3 0.0 copy-done.2
  279.3 8.7 %fusion.22 = f32[64,192]{1,0:T(8,128)S(1)} fusion(bf16[64,32768]{1,0:T(8,128)(2,1)S(1)} %copy-done.2, bf16[192,32768]{1,0:T(8,128)(2,1)} %all-gather.2.cloned.1.call-done), kind=kOutput, calls=%fused_computation.44 | convolution fusion | flops 805306368 | bytes 16826368 | tf_op jit(solution)/shard_map/dot_general | solution.py:33
  288.0 0.3 fusion.21
  288.3 0.2 fusion.8
  288.5 0.1 fusion.19
  288.6 68.2 %all_gather.7 = bf16[512,192]{1,0:T(8,128)(2,1)S(1)} all-gather(bf16[64,192]{1,0:T(8,128)(2,1)S(1)} %get-tuple-element.5), channel_id=1, replica_groups=mesh['grp'=8,'blk'=4] {'grp'}, dimensions={0}, use_global_device_ids=true | all-gather | bytes 221184 | tf_op jit(solution)/shard_map/all_gather | solution.py:46
  356.8 0.0 all-to-all-done.2
  356.8 4.9 %fusion.23 = f32[192,4096]{1,0:T(8,128)} fusion(bf16[512,192]{1,0:T(8,128)(2,1)S(1)} %all_gather.7, bf16[512,4096]{1,0:T(8,128)(2,1)} %bitcast.11), kind=kOutput, calls=%fused_computation.45 | convolution fusion | flops 805306368 | bytes 7536640 | tf_op jit(solution)/shard_map/dot_general | solution.py:48
  361.7 0.0 reduce-scatter.2.cloned.1.call-update
  361.7 0.2 fusion.10
  362.0 39.1 %psum.7 = f32[192,8]{0,1:T(8,128)S(1)} all-reduce(f32[192,8]{0,1:T(8,128)S(1)} %fusion.10), channel_id=1, replica_groups=mesh['grp'=8,'blk'=4] {'grp','blk'}, use_global_device_ids=true, to_apply=%region_6.7 | all-reduce | flops 1536 | bytes 12288 | tf_op jit(solution)/shard_map/psum | solution.py:42
  401.1 4.8 %reduce-scatter.2.cloned.1.call-done = f32[48,4096]{1,0:T(8,128)} async-done(((f32[192,4096]{1,0:T(8,128)}), f32[48,4096]{1,0:T(8,128)}) %reduce-scatter.2.cloned.1.call-update) | async-done | bytes 786448 | tf_op jit(solution)/shard_map/reduce_scatter | solution.py:47
  405.8 2.9 fusion.4
  (4 shorter events, 0.0 us)
Async XLA Ops:
  6.5 234.9 %copy-start = (f32[8,32768]{1,0:T(8,128)S(1)}, f32[8,32768]{1,0:T(8,128)}, u32[]{:S(2)}) copy-start(f32[8,32768]{1,0:T(8,128)} %param.13) | copy-start | bytes 3145732
  19.7 9.8 %all-to-all-start = ((s32[4,1,32]{2,1,0:T(1,128)}), s32[4,1,32]{2,1,0:T(1,128)S(1)}, u32[]{:S(2)}, u32[]{:S(2)}) async-start(s32[4,1,32]{2,1,0:T(1,128)} %bitcast.4), calls=%async_computation | async-start | bytes 4096 | tf_op jit(solution)/shard_map/all_to_all | solution.py:20
  24.9 231.8 %all-gather.2.cloned.1.call-start = ((), (), s32[]{:S(2)}) async-start(), calls=%async_computation.4 | async-start | bytes 15728640 | tf_op jit(solution)/shard_map/all_gather | solution.py:32
  229.3 12.2 %copy-start.3 = (s32[64]{0:T(128)S(1)}, s32[64]{0:T(128)}, u32[]{:S(2)}) copy-start(s32[64]{0:T(128)} %param.10) | copy-start | bytes 772
  247.0 2.0 copy-start.1
  251.2 105.6 %all-to-all-start.2 = ((bf16[64,8,4096]{2,0,1:T(8,128)(2,1)}), bf16[64,8,4096]{2,0,1:T(8,128)(2,1)}, u32[]{:S(2)}, u32[]{:S(2)}) async-start(bf16[64,8,4096]{2,0,1:T(8,128)(2,1)} %bitcast.37), calls=%async_computation.2 | async-start | bytes 8388608 | tf_op jit(solution)/shard_map/all_to_all | solution.py:45
  255.8 150.1 %reduce-scatter.2.cloned.1.call-start = ((), (), s32[]{:S(2)}) async-start(), calls=%async_computation.5 | async-start | bytes 3932160 | tf_op jit(solution)/shard_map/reduce_scatter | solution.py:47
  256.7 22.6 %copy-start.2 = (bf16[64,32768]{1,0:T(8,128)(2,1)S(1)}, bf16[64,32768]{1,0:T(8,128)(2,1)}, u32[]{:S(2)}) copy-start(bf16[64,32768]{1,0:T(8,128)(2,1)} %copy-done.1) | copy-start | bytes 12582916
Sparse Core Ops, SparseCore 0:
  27.5 206.4 all-gather.1
  361.8 43.9 reduce-scatter.1
where the time goes:
time: 416 us
  blocking collectives  279 us (67%)
  local copies, waits for them, and re-layouts  46.8 us (11%)
  matrix products  45.2 us (11%)
  between operations  14.1 us (3%)
  other arithmetic  10.8 us (3%)
  starting transfers between devices  10 us (2%)
  waiting for transfers between devices  9.39 us (2%)
    all_to_all x1, blocking collectives, per_device(): lax.all_to_all(blocks_out, 'blk', split_axis=0, concat_axis=0, tiled=True)  172 us
    all_gather x1, blocking collectives, per_device(): all_weights = lax.all_gather(weighted_b, 'grp', axis=0, tiled=True)  68.2 us
    psum x1, blocking collectives, per_device(): lax.psum(jnp.dot(weighted.T, masks_hot, precision=highest), ('grp', 'blk'))  39.1 us
    dot_general x1, matrix products, per_device(): jnp.dot(wedge, (piece_float * piece_float).T, precision=highest)  22.6 us
    gather x1, local copies, waits for them, and re-layouts, per_device(): jnp.take(slab, wanted.reshape(-1), axis=0)  19.2 us
    gather x1, local copies, waits for them, and re-layouts, per_device(): blocks = fetched[owners, slot_rank]  12.2 us
    scatter x1, local copies, waits for them, and re-layouts, per_device(): jnp.zeros((cycle_size, capacity), jnp.int32).at[owners, slot_rank]  10.1 us
    dot_general x1, matrix products, per_device(): correl = jnp.dot(scaled, ref_piece.T, preferred_element_type=jnp.float32)  8.69 us
  transfers between devices with their start and end apart: 4, of which 2 were waited for; matrix products, arithmetic and copies ran while one was open for 19% of the time, Pallas kernels for 0%

commit v1 on v0

--- a/solution.py
+++ b/solution.py
@@ -39,7 +39,9 @@
     live_mask = (jnp.arange(slot_count, dtype=jnp.int32) < live_count[0]).astype(jnp.float32)
     weighted = posterior * live_mask[:, None]
     weighted_b = weighted.astype(jnp.bfloat16)
-    totals = lax.psum(jnp.dot(weighted.T, masks_hot, precision=highest), ("grp", "blk"))
+    totals = jnp.dot(weighted.T, masks_hot, precision=highest)
+    for over in ("blk", "grp"):
+        totals = lax.psum(totals, over)
     per_vox = voxels // group_count
     contract = (((0,), (0,)), ((), ()))
     columns = lax.all_to_all(scaled, "grp", split_axis=1, concat_axis=0, tiled=True)

time: 416 us -> 416 us (level)
  blocking collectives: 279 us -> 263 us
  waiting for transfers between devices: 9.39 us -> 24.3 us
    psum x1 -> x2, blocking collectives: 39.1 us -> 23.4 us  [per_device(): totals = lax.psum(totals, over)]
    reduce_scatter x1, waiting for transfers between devices: 4.76 us -> 19.7 us  [per_device(): lax.psum_scatter(lax.dot_general(all_weights, columns, contract, preferre...]
where the time goes in v1:
time: 416 us; the launch traced here: 415 us
  blocking collectives  263 us (63%)
  local copies, waits for them, and re-layouts  46.8 us (11%)
  matrix products  45.2 us (11%)
  waiting for transfers between devices  24.3 us (6%)
  between operations  14.2 us (3%)
  other arithmetic  10.8 us (3%)
  starting transfers between devices  10 us (2%)
    all_to_all x1, blocking collectives, per_device(): lax.all_to_all(blocks_out, 'blk', split_axis=0, concat_axis=0, tiled=True)  172 us
    all_gather x1, blocking collectives, per_device(): all_weights = lax.all_gather(weighted_b, 'grp', axis=0, tiled=True)  68.2 us
    psum x2, blocking collectives, per_device(): totals = lax.psum(totals, over)  23.4 us
    dot_general x1, matrix products, per_device(): jnp.dot(wedge, (piece_float * piece_float).T, precision=highest)  22.6 us
    reduce_scatter x1, waiting for transfers between devices, per_device(): lax.psum_scatter(lax.dot_general(all_weights, columns, contract, preferre...  19.7 us
    gather x1, local copies, waits for them, and re-layouts, per_device(): jnp.take(slab, wanted.reshape(-1), axis=0)  19.2 us
    gather x1, local copies, waits for them, and re-layouts, per_device(): blocks = fetched[owners, slot_rank]  12.2 us
    scatter x1, local copies, waits for them, and re-layouts, per_device(): jnp.zeros((cycle_size, capacity), jnp.int32).at[owners, slot_rank]  10.1 us
  transfers between devices with their start and end apart: 4, of which 2 were waited for; matrix products, arithmetic and copies ran while one was open for 19% of the time, Pallas kernels for 0%

profile of v1, /device:TPU:0, one launch (start us, length us, event | category | flops | bytes accessed | tf_op | source)
XLA Modules:
  0.0 414.9 jit_solution(16535165400571054729)
XLA Ops:
  6.5 0.0 copy-start
  6.5 0.8 fusion.9
  7.4 0.1 reduce_window_sum.11
  7.4 0.8 select_reduce_fusion
  8.3 0.7 fusion.18
  9.0 0.6 broadcast_in_dim.12
  9.5 10.1 %scatter_fusion = s32[4,32]{1,0:T(4,128)} fusion(s32[4,32]{1,0:T(4,128)} %broadcast_in_dim.12, s32[64]{0:T(128)S(1)} %get-tuple-element.7, s32[64]{0:T(128)} %param.9), kind=kCustom, calls=%fused_computation.2 | custom fusion | bytes 1280 | tf_op jit(solution)/shard_map/scatter | solution.py:19
  19.7 5.2 %all-to-all-start = ((s32[4,1,32]{2,1,0:T(1,128)}), s32[4,1,32]{2,1,0:T(1,128)S(1)}, u32[]{:S(2)}, u32[]{:S(2)}) async-start(s32[4,1,32]{2,1,0:T(1,128)} %bitcast.4), calls=%async_computation | async-start | bytes 4096 | tf_op jit(solution)/shard_map/all_to_all | solution.py:20
  24.9 0.0 all-gather.2.cloned.1.call-start
  24.9 0.7 all-gather.2.cloned.1.call-update
  25.6 3.9 all-to-all-done
  29.5 0.5 broadcast.140
  30.0 0.7 reduce.3
  30.6 0.1 reshape.75
  30.7 19.2 %gather_fusion = bf16[128,32768]{1,0:T(8,128)(2,1)} fusion(bf16[64,32768]{1,0:T(8,128)(2,1)} %param.7, s32[1024]{0:T(1024)S(1)} %pad_clamp_fusion), kind=kCustom, calls=%fused_computation | custom fusion | bytes 16777728 | tf_op jit(solution)/shard_map/jit(_take)/gather | solution.py:22
  49.9 7.4 %broadcast_select_fusion = bf16[4,32,32768]{2,1,0:T(8,128)(2,1)} fusion(bf16[4,32,32768]{2,1,0:T(8,128)(2,1)} %bitcast.36, pred[4,32]{1,0:T(4,128)(4,1)S(1)} %compare_and_fusion), kind=kLoop, calls=%fused_computation.8 | loop fusion | flops 4194304 | bytes 16777344 | tf_op jit(solution)/shard_map/jit(_take)/select_n | solution.py:22
  57.4 171.9 %all_to_all.33 = bf16[4,32,32768]{2,1,0:T(8,128)(2,1)} all-to-all(bf16[4,32,32768]{2,1,0:T(8,128)(2,1)} %broadcast_select_fusion), channel_id=1, replica_groups=mesh['grp'=8,'blk'=4] {'blk'}, dimensions={0} | all-to-all | bytes 16777216 | tf_op jit(solution)/shard_map/all_to_all | solution.py:23
  229.3 0.0 copy-start.3
  229.3 12.2 %gather_fusion.1 = bf16[64,32768]{1,0:T(8,128)(2,1)} fusion(bf16[4,32,32768]{2,1,0:T(8,128)(2,1)} %all_to_all.33, s32[64]{0:T(128)S(1)} %bitcast.38), kind=kCustom, calls=%fused_computation.1 | custom fusion | bytes 8389120 | tf_op jit(solution)/shard_map/gather | solution.py:24
  241.5 0.0 copy-done
  241.5 0.0 copy-done.3
  241.5 5.5 %fusion = bf16[64,32768]{1,0:T(8,128)(2,1)S(1)} fusion(f32[8,32768]{1,0:T(8,128)S(1)} %copy-done, bf16[64,32768]{1,0:T(8,128)(2,1)} %gather_fusion.1, s32[64]{0:T(128)S(1)} %copy-done.3), kind=kOutput, calls=%fused_computation.4 | convolution fusion | flops 207618560 | bytes 9437440 | tf_op jit(solution)/shard_map/dot_general | solution.py:28
  247.0 0.0 copy-start.1
  247.0 2.0 copy-done.1
  249.0 2.2 copy.13
  251.2 4.6 %all-to-all-start.2 = ((bf16[64,8,4096]{2,0,1:T(8,128)(2,1)}), bf16[64,8,4096]{2,0,1:T(8,128)(2,1)}, u32[]{:S(2)}, u32[]{:S(2)}) async-start(bf16[64,8,4096]{2,0,1:T(8,128)(2,1)} %bitcast.37), calls=%async_computation.2 | async-start | bytes 8388608 | tf_op jit(solution)/shard_map/all_to_all | solution.py:47
  255.8 0.3 reduce-scatter.2.cloned.1.call-start
  256.7 0.0 all-gather.2.cloned.1.call-done
  256.7 0.0 copy-start.2
  256.7 22.6 %fusion.1 = f32[192,8]{0,1:T(8,128)S(1)} fusion(f32[8,32768]{1,0:T(8,128)S(1)} %copy-done, bf16[192,32768]{1,0:T(8,128)(2,1)} %all-gather.2.cloned.1.call-done), kind=kOutput, calls=%fused_computation.5 | convolution fusion | flops 616562688 | bytes 13637632 | tf_op jit(solution)/shard_map/dot_general | solution.py:35
  279.3 0.0 copy-done.2
  279.3 8.7 %fusion.22 = f32[64,192]{1,0:T(8,128)S(1)} fusion(bf16[64,32768]{1,0:T(8,128)(2,1)S(1)} %copy-done.2, bf16[192,32768]{1,0:T(8,128)(2,1)} %all-gather.2.cloned.1.call-done), kind=kOutput, calls=%fused_computation.44 | convolution fusion | flops 805306368 | bytes 16826368 | tf_op jit(solution)/shard_map/dot_general | solution.py:33
  288.0 0.3 fusion.21
  288.3 0.2 fusion.8
  288.5 0.1 fusion.19
  288.6 68.2 %all_gather.7 = bf16[512,192]{1,0:T(8,128)(2,1)S(1)} all-gather(bf16[64,192]{1,0:T(8,128)(2,1)S(1)} %get-tuple-element.5), channel_id=1, replica_groups=mesh['grp'=8,'blk'=4] {'grp'}, dimensions={0}, use_global_device_ids=true | all-gather | bytes 221184 | tf_op jit(solution)/shard_map/all_gather | solution.py:48
  356.8 0.0 all-to-all-done.2
  356.8 4.9 %fusion.23 = f32[192,4096]{1,0:T(8,128)} fusion(bf16[512,192]{1,0:T(8,128)(2,1)S(1)} %all_gather.7, bf16[512,4096]{1,0:T(8,128)(2,1)} %bitcast.11), kind=kOutput, calls=%fused_computation.45 | convolution fusion | flops 805306368 | bytes 7536640 | tf_op jit(solution)/shard_map/dot_general | solution.py:50
  361.7 0.0 reduce-scatter.2.cloned.1.call-update
  361.7 0.2 fusion.10
  362.0 9.2 %psum.14 = f32[192,8]{0,1:T(8,128)S(1)} all-reduce(f32[192,8]{0,1:T(8,128)S(1)} %fusion.10), channel_id=1, replica_groups=mesh['grp'=8,'blk'=4] {'blk'}, use_global_device_ids=true, to_apply=%region_6.7 | all-reduce | flops 1536 | bytes 12288 | tf_op jit(solution)/shard_map/psum | solution.py:44
  371.1 14.2 %psum.15 = f32[192,8]{0,1:T(8,128)S(1)} all-reduce(f32[192,8]{0,1:T(8,128)S(1)} %psum.14), channel_id=1, replica_groups=mesh['grp'=8,'blk'=4] {'grp'}, use_global_device_ids=true, to_apply=%region_7.8 | all-reduce | flops 1536 | bytes 12288 | tf_op jit(solution)/shard_map/psum | solution.py:44
  385.4 19.7 %reduce-scatter.2.cloned.1.call-done = f32[48,4096]{1,0:T(8,128)} async-done(((f32[192,4096]{1,0:T(8,128)}), f32[48,4096]{1,0:T(8,128)}) %reduce-scatter.2.cloned.1.call-update) | async-done | bytes 786448 | tf_op jit(solution)/shard_map/reduce_scatter | solution.py:49
  405.1 2.9 fusion.4
  (4 shorter events, 0.0 us)
Async XLA Ops:
  6.5 234.9 %copy-start = (f32[8,32768]{1,0:T(8,128)S(1)}, f32[8,32768]{1,0:T(8,128)}, u32[]{:S(2)}) copy-start(f32[8,32768]{1,0:T(8,128)} %param.13) | copy-start | bytes 3145732
  19.7 9.8 %all-to-all-start = ((s32[4,1,32]{2,1,0:T(1,128)}), s32[4,1,32]{2,1,0:T(1,128)S(1)}, u32[]{:S(2)}, u32[]{:S(2)}) async-start(s32[4,1,32]{2,1,0:T(1,128)} %bitcast.4), calls=%async_computation | async-start | bytes 4096 | tf_op jit(solution)/shard_map/all_to_all | solution.py:20
  24.9 231.8 %all-gather.2.cloned.1.call-start = ((), (), s32[]{:S(2)}) async-start(), calls=%async_computation.4 | async-start | bytes 15728640 | tf_op jit(solution)/shard_map/all_gather | solution.py:32
  229.3 12.2 %copy-start.3 = (s32[64]{0:T(128)S(1)}, s32[64]{0:T(128)}, u32[]{:S(2)}) copy-start(s32[64]{0:T(128)} %param.10) | copy-start | bytes 772
  247.0 2.0 copy-start.1
  251.2 105.6 %all-to-all-start.2 = ((bf16[64,8,4096]{2,0,1:T(8,128)(2,1)}), bf16[64,8,4096]{2,0,1:T(8,128)(2,1)}, u32[]{:S(2)}, u32[]{:S(2)}) async-start(bf16[64,8,4096]{2,0,1:T(8,128)(2,1)} %bitcast.37), calls=%async_computation.2 | async-start | bytes 8388608 | tf_op jit(solution)/shard_map/all_to_all | solution.py:47
  255.8 149.3 %reduce-scatter.2.cloned.1.call-start = ((), (), s32[]{:S(2)}) async-start(), calls=%async_computation.5 | async-start | bytes 3932160 | tf_op jit(solution)/shard_map/reduce_scatter | solution.py:49
  256.7 22.6 %copy-start.2 = (bf16[64,32768]{1,0:T(8,128)(2,1)S(1)}, bf16[64,32768]{1,0:T(8,128)(2,1)}, u32[]{:S(2)}) copy-start(bf16[64,32768]{1,0:T(8,128)(2,1)} %copy-done.1) | copy-start | bytes 12582916
Sparse Core Ops, SparseCore 0:
  27.5 206.4 all-gather.1
  361.8 43.2 reduce-scatter.1
